TPU v7x, 32 devices: a whole 2x2x4 slice. The times are simulated.
32 devices in a mesh: section: 4 (over y, x), expert: 8 (over z, core).
Axes of the slice: x: 2, y: 2, z: 4, core: 2. Of those that a mesh axis runs over, the one named last changes fastest.
Arguments:
- tokens: bfloat16 [2, 256, 7168], P(None, 'expert'), may hold values from -6 to 6
- norm_gain: float32 [4, 7168], P('section'), may hold values from 0.25 to 1.75
- w_gate: bfloat16 [4, 7168, 2048], P('section', None, 'expert'), may hold values from -0.0625 to 0.0625
- w_up: bfloat16 [4, 7168, 2048], P('section', None, 'expert'), may hold values from -0.0625 to 0.0625
- w_down: bfloat16 [4, 2048, 7168], P('section', 'expert'), may hold values from -0.1875 to 0.1875
- expert_ids: int32 [4, 2, 256, 1], P('section', None, 'expert'), may hold values from 0 to 1; in each aligned block of 32 rows (0 to 31, 32 to 63, ..., all dimensions but the last counted through in order) at most 24 rows name the same one
- gate_weight: float32 [4, 2, 256, 1], P('section', None, 'expert'), may hold values from 0.3 to 1.5
- capacity: int32 [4, 2], P('section'), may hold values from 64 to 192
Outputs:
- results: bfloat16 [2, 256, 7168], P(None, 'expert', 'section')
Inputs may be any that keep to these rules, and one draw needn't show every extreme that they name: `expert_ids`: A token's 1 expert differ. In each aligned block of 32 tokens (the tokens of one device in one span and layer) no expert is named by more than 24 tokens, a bound that some block reaches.
All inputs are finite; a program needn't handle non-finite values.
Results may differ from a plain program's by a relative error of at most 0.0095.
Values may be sent and summed in bfloat16 or wider, within the bound.
No kernel may reach another device: no remote copies, remote signals or barrier semaphores. Data moves between devices by JAX's collectives and lax.ppermute only.
A program may use at most 128 MiB of HBM per device.

v0:
```python
import jax
import jax.numpy as jnp
from jax import lax
from jax.sharding import PartitionSpec as P

EPSILON = 1e-06


def entering(array, axis, combine, identity):
    length, place = (lax.axis_size(axis), lax.axis_index(axis))
    everything = lax.all_gather(array, axis)
    start = jnp.broadcast_to(jnp.asarray(identity, array.dtype), array.shape)

    def hop(k, before):
        reached = k < place
        new = combine(before, everything[k])
        return jnp.where(reached, new, before)

    return lax.fori_loop(0, length, hop, start)


def shifted(array, axis, by):
    length = lax.axis_size(axis)
    pairs = [(i, i + by) for i in range(length) if 0 <= i + by < length]
    return lax.ppermute(array, axis, pairs)


def slot_numbers(routed):
    length = routed.shape[-1]
    order = jnp.arange(length, dtype=jnp.int32)
    earlier = order[:, None] > order[None, :]
    alike = routed[..., :, None] == routed[..., None, :]
    return jnp.sum((alike & earlier).astype(jnp.int32), axis=-1)


def add_counts(earlier_counts, later_counts):
    return earlier_counts + later_counts


def expert_rows(arrived, gate_cols, up_cols, down_rows):
    width = arrived.shape[-1]
    flat_rows = arrived.reshape(-1, width)
    gate_out = jnp.dot(flat_rows, gate_cols, preferred_element_type=jnp.float32)
    up_out = jnp.dot(flat_rows, up_cols, preferred_element_type=jnp.float32)
    hidden = (jax.nn.silu(gate_out) * up_out).astype(jnp.bfloat16)
    partial_out = jnp.dot(hidden, down_rows, preferred_element_type=jnp.float32).astype(
        jnp.bfloat16
    )
    return partial_out.reshape(arrived.shape)


def moe_layer(
    stream, gain, gate_cols, up_cols, down_rows, routed_ids, gate_values, limits, slot_count
):
    token_rows, width = stream.shape
    top_count = routed_ids.shape[-1]
    expert_total = limits.shape[0]
    device_count = lax.axis_size("expert")
    split_count = device_count // expert_total
    widened = stream.astype(jnp.float32)
    stats = jnp.mean(widened * widened, axis=-1, keepdims=True)
    normed = (widened * lax.rsqrt(stats + EPSILON) * gain[None, :]).astype(jnp.bfloat16)
    flat_ids = routed_ids.reshape(-1)
    slots = slot_numbers(flat_ids)
    expert_iota = jnp.arange(expert_total, dtype=jnp.int32)
    onehot_ids = (flat_ids[:, None] == expert_iota[None, :]).astype(jnp.int32)
    counts = jnp.sum(onehot_ids, axis=0)
    before = entering(counts, "expert", add_counts, jnp.zeros_like(counts))
    queue = jnp.sum(onehot_ids * before[None, :], axis=1) + slots
    bound = jnp.sum(onehot_ids * limits[None, :], axis=1)
    weights = jnp.where(queue < bound, gate_values.reshape(-1), jnp.float32(0.0))
    target = flat_ids * slot_count + slots
    buffer_iota = jnp.arange(expert_total * slot_count, dtype=jnp.int32)
    placed = (buffer_iota[None, :] == target[:, None]).astype(jnp.float32)
    select = jnp.sum(placed.reshape(token_rows, top_count, -1), axis=1).astype(jnp.bfloat16)
    packed = lax.dot_general(
        select, normed, (((0,), (0,)), ((), ())), preferred_element_type=jnp.float32
    ).astype(jnp.bfloat16)
    outgoing = jnp.repeat(packed.reshape(expert_total, slot_count, width), split_count, axis=0)
    partials = expert_rows(
        lax.all_to_all(outgoing, "expert", split_axis=0, concat_axis=0, tiled=True),
        gate_cols,
        up_cols,
        down_rows,
    )
    returned = lax.all_to_all(partials, "expert", split_axis=0, concat_axis=0, tiled=True)
    summed = jnp.sum(
        returned.reshape(expert_total, split_count, slot_count, width).astype(jnp.float32), axis=1
    ).reshape(-1, width)
    mixing = jnp.sum((placed * weights[:, None]).reshape(token_rows, top_count, -1), axis=1)
    moe_out = jnp.dot(
        mixing, summed, precision=lax.Precision.HIGHEST, preferred_element_type=jnp.float32
    )
    return (widened + moe_out).astype(jnp.bfloat16)


def body(tokens, norm_gain, w_gate, w_up, w_down, expert_ids, gate_weight, capacity):
    section_count = lax.axis_size("section")
    section_index = lax.axis_index("section")
    span_count, token_rows, width = tokens.shape
    top_count = expert_ids.shape[-1]
    expert_total = capacity.shape[-1]
    slot_count = min(token_rows, max(2, 3 * (token_rows * top_count) // (2 * expert_total)))
    held = jnp.zeros((token_rows, width), jnp.bfloat16)
    results = jnp.zeros((span_count, token_rows, width), jnp.bfloat16)
    moments = section_count + span_count - 1
    for moment in range(moments):
        position = moment - section_index
        active = (position >= 0) & (position < span_count)
        picked = jnp.clip(position, 0, span_count - 1)
        entry = tokens[min(moment, span_count - 1)]
        stream = jnp.where(section_index == 0, entry, held)
        routed = lax.dynamic_index_in_dim(expert_ids[0], picked, 0, keepdims=False)
        gates = lax.dynamic_index_in_dim(gate_weight[0], picked, 0, keepdims=False)
        layer_out = moe_layer(
            stream,
            norm_gain[0],
            w_gate[0],
            w_up[0],
            w_down[0],
            routed,
            gates,
            capacity[0],
            slot_count,
        )
        finished = active & (section_index == section_count - 1)
        results = jnp.where(
            finished, lax.dynamic_update_index_in_dim(results, layer_out, picked, 0), results
        )
        if moment + 1 < moments:
            held = shifted(layer_out, "section", 1)
    collected = lax.psum_scatter(
        results.astype(jnp.float32).astype(jnp.bfloat16), "section", scatter_dimension=2, tiled=True
    )
    return collected


def solution(mesh):
    in_specs = (
        P(None, "expert", None),
        P("section", None),
        P("section", None, "expert"),
        P("section", None, "expert"),
        P("section", "expert", None),
        P("section", None, "expert", None),
        P("section", None, "expert", None),
        P("section", None),
    )
    out_specs = P(None, "expert", "section")
    return jax.shard_map(body, mesh=mesh, in_specs=in_specs, out_specs=out_specs, check_vma=False)
```

profile of v0, /device:TPU:0, one launch (start us, length us, event | category | flops | bytes accessed | tf_op | source)
XLA Modules:
  0.0 837.8 jit_solution(17388975175286004267)
XLA Ops:
  6.5 0.8 fusion.151
  7.5 1.2 fusion.74
  8.8 1.5 convolution_convert_fusion.9
  10.3 1.9 broadcast_in_dim.41
  12.2 6.5 all-to-all-start
  18.7 0.6 dynamic-slice.20
  21.5 60.4 %all-reduce.5 = (s32[16]{0:T(128)S(1)}, s32[16]{0:T(128)S(1)}, s32[16]{0:T(128)S(1)}, s32[16]{0:T(128)S(1)}, s32[16]{0:T(128)S(1)}) all-reduce(s32[16]{0:T(128)S(1)} %dynamic-update-slice.9, s32[16]{0:T(128)S(1)} %dynamic-update-slice.6, s32[16]{0:T(128)S(1)} %dynamic-update-slice.7, ...), channel_id=6, replica_groups=mesh['section'=4,'expert'=8] {'expert'}, use_global_device_ids=true, to_apply=%add.4 | all-reduce | flops 80 | bytes 640
  82.2 0.3 while.70
  82.5 0.3 while.71
  82.8 2.9 fusion.31
  85.7 7.8 convolution_convert_fusion.4
  93.5 3.8 all-to-all-start.1
  97.3 0.3 while.72
  98.0 0.3 while.73
  98.3 0.3 while.74
  98.9 61.4 %all-to-all-done.1 = bf16[8,24,7168]{2,1,0:T(8,128)(2,1)S(1)} async-done(((bf16[8,24,7168]{2,1,0:T(8,128)(2,1)}), bf16[8,24,7168]{2,1,0:T(8,128)(2,1)S(1)}, u32[]{:S(2)}, u32[]{:S(2)}) %all-to-all-start.1) | async-done | bytes 2752544 | tf_op jit(solution)/shard_map/all_to_all | solution.py:86
  160.3 0.4 convert_reduce_fusion.4
  160.7 1.0 broadcast_in_dim.38
  161.7 1.7 bitcast_dynamic-update-slice_fusion
  163.5 3.4 collective-permute-start
  166.9 9.4 %collective-permute-done = bf16[32,7168]{1,0:T(8,128)(2,1)S(1)} collective-permute-done((bf16[32,7168]{1,0:T(8,128)(2,1)S(1)}, bf16[32,7168]{1,0:T(8,128)(2,1)S(1)}, u32[]{:S(2)}, u32[]{:S(2)}) %collective-permute-start) | collective-permute-done | bytes 458784 | tf_op jit(solution)/shard_map/ppermute | solution.py:25
  176.6 0.4 convolution_convert_fusion.8
  177.0 0.3 broadcast_in_dim.43
  177.4 66.2 %all_to_all.50 = bf16[8,24,7168]{2,1,0:T(8,128)(2,1)S(1)} all-to-all(bf16[8,24,7168]{2,1,0:T(8,128)(2,1)S(1)} %bitcast.240), channel_id=1, replica_groups=mesh['section'=4,'expert'=8] {'expert'}, dimensions={0} | all-to-all | bytes 5505024 | tf_op jit(solution)/shard_map/all_to_all | solution.py:81
  243.5 0.9 fusion.29
  244.5 7.8 convolution_convert_fusion.3
  252.3 3.6 all-to-all-start.3
  256.1 62.9 %all-to-all-done.3 = bf16[8,24,7168]{2,1,0:T(8,128)(2,1)S(1)} async-done(((bf16[8,24,7168]{2,1,0:T(8,128)(2,1)}), bf16[8,24,7168]{2,1,0:T(8,128)(2,1)S(1)}, u32[]{:S(2)}, u32[]{:S(2)}) %all-to-all-start.3) | async-done | bytes 2752544 | tf_op jit(solution)/shard_map/all_to_all | solution.py:86
  318.9 0.4 convert_reduce_fusion.3
  319.3 2.8 fusion.97
  322.1 4.4 collective-permute-start.1
  326.6 9.4 %collective-permute-done.1 = bf16[32,7168]{1,0:T(8,128)(2,1)S(1)} collective-permute-done((bf16[32,7168]{1,0:T(8,128)(2,1)S(1)}, bf16[32,7168]{1,0:T(8,128)(2,1)S(1)}, u32[]{:S(2)}, u32[]{:S(2)}) %collective-permute-start.1) | collective-permute-done | bytes 458784 | tf_op jit(solution)/shard_map/ppermute | solution.py:25
  336.3 0.4 convolution_convert_fusion.7
  336.7 0.3 broadcast_in_dim.45
  337.0 66.2 %all_to_all.51 = bf16[8,24,7168]{2,1,0:T(8,128)(2,1)S(1)} all-to-all(bf16[8,24,7168]{2,1,0:T(8,128)(2,1)S(1)} %bitcast.241), channel_id=1, replica_groups=mesh['section'=4,'expert'=8] {'expert'}, dimensions={0} | all-to-all | bytes 5505024 | tf_op jit(solution)/shard_map/all_to_all | solution.py:81
  403.2 0.9 fusion.27
  404.2 7.8 convolution_convert_fusion.2
  412.0 3.6 all-to-all-start.5
  415.8 62.9 %all-to-all-done.5 = bf16[8,24,7168]{2,1,0:T(8,128)(2,1)S(1)} async-done(((bf16[8,24,7168]{2,1,0:T(8,128)(2,1)}), bf16[8,24,7168]{2,1,0:T(8,128)(2,1)S(1)}, u32[]{:S(2)}, u32[]{:S(2)}) %all-to-all-start.5) | async-done | bytes 2752544 | tf_op jit(solution)/shard_map/all_to_all | solution.py:86
  478.6 0.4 convert_reduce_fusion.2
  479.0 2.8 fusion.96
  481.8 4.4 collective-permute-start.2
  486.4 9.3 %collective-permute-done.2 = bf16[32,7168]{1,0:T(8,128)(2,1)S(1)} collective-permute-done((bf16[32,7168]{1,0:T(8,128)(2,1)S(1)}, bf16[32,7168]{1,0:T(8,128)(2,1)S(1)}, u32[]{:S(2)}, u32[]{:S(2)}) %collective-permute-start.2) | collective-permute-done | bytes 458784 | tf_op jit(solution)/shard_map/ppermute | solution.py:25
  495.9 0.4 convolution_convert_fusion.6
  496.4 0.3 broadcast_in_dim.47
  496.7 66.2 %all_to_all.52 = bf16[8,24,7168]{2,1,0:T(8,128)(2,1)S(1)} all-to-all(bf16[8,24,7168]{2,1,0:T(8,128)(2,1)S(1)} %bitcast.242), channel_id=1, replica_groups=mesh['section'=4,'expert'=8] {'expert'}, dimensions={0} | all-to-all | bytes 5505024 | tf_op jit(solution)/shard_map/all_to_all | solution.py:81
  562.9 0.9 fusion.25
  563.8 7.8 convolution_convert_fusion.1
  571.6 3.6 all-to-all-start.7
  575.4 62.8 %all-to-all-done.7 = bf16[8,24,7168]{2,1,0:T(8,128)(2,1)S(1)} async-done(((bf16[8,24,7168]{2,1,0:T(8,128)(2,1)}), bf16[8,24,7168]{2,1,0:T(8,128)(2,1)S(1)}, u32[]{:S(2)}, u32[]{:S(2)}) %all-to-all-start.7) | async-done | bytes 2752544 | tf_op jit(solution)/shard_map/all_to_all | solution.py:86
  638.3 0.4 convert_reduce_fusion.1
  638.7 2.8 fusion.95
  641.4 5.2 collective-permute-start.3
  646.7 9.4 %collective-permute-done.3 = bf16[32,7168]{1,0:T(8,128)(2,1)S(1)} collective-permute-done((bf16[32,7168]{1,0:T(8,128)(2,1)S(1)}, bf16[32,7168]{1,0:T(8,128)(2,1)S(1)}, u32[]{:S(2)}, u32[]{:S(2)}) %collective-permute-start.3) | collective-permute-done | bytes 458784 | tf_op jit(solution)/shard_map/ppermute | solution.py:25
  656.4 0.5 convolution_convert_fusion.5
  656.9 0.3 broadcast_in_dim.49
  657.2 66.2 %all_to_all.53 = bf16[8,24,7168]{2,1,0:T(8,128)(2,1)S(1)} all-to-all(bf16[8,24,7168]{2,1,0:T(8,128)(2,1)S(1)} %bitcast.243), channel_id=1, replica_groups=mesh['section'=4,'expert'=8] {'expert'}, dimensions={0} | all-to-all | bytes 5505024 | tf_op jit(solution)/shard_map/all_to_all | solution.py:81
  723.4 0.9 fusion.23
  724.3 7.8 convolution_convert_fusion
  732.1 3.6 all-to-all-start.9
  735.9 62.8 %all-to-all-done.9 = bf16[8,24,7168]{2,1,0:T(8,128)(2,1)S(1)} async-done(((bf16[8,24,7168]{2,1,0:T(8,128)(2,1)}), bf16[8,24,7168]{2,1,0:T(8,128)(2,1)S(1)}, u32[]{:S(2)}, u32[]{:S(2)}) %all-to-all-start.9) | async-done | bytes 2752544 | tf_op jit(solution)/shard_map/all_to_all | solution.py:86
  798.7 0.4 convert_reduce_fusion
  799.2 2.7 fusion.7
  801.9 29.0 %reduce-scatter.2.cloned.1.call-done = bf16[2,32,1792]{2,1,0:T(8,128)(2,1)} async-done(((bf16[2,32,7168]{2,1,0:T(8,128)(2,1)}), bf16[2,32,1792]{2,1,0:T(8,128)(2,1)}) %reduce-scatter.2.cloned.1.call-update) | async-done | bytes 229392 | tf_op jit(solution)/shard_map/reduce_scatter | solution.py:132
  (115 shorter events, 5.2 us)
Async XLA Ops:
  12.2 6.5 copy-start.11
  12.2 70.6 %all-to-all-start = ((bf16[8,24,7168]{2,1,0:T(8,128)(2,1)}), bf16[8,24,7168]{2,1,0:T(8,128)(2,1)S(1)}, u32[]{:S(2)}, u32[]{:S(2)}) async-start(bf16[8,24,7168]{2,1,0:T(8,128)(2,1)} %bitcast.235), calls=%async_computation | async-start | bytes 5505024 | tf_op jit(solution)/shard_map/all_to_all | solution.py:81
  93.5 5.1 copy-start.10
  93.5 5.2 copy-start.9
  93.5 66.8 %all-to-all-start.1 = ((bf16[8,24,7168]{2,1,0:T(8,128)(2,1)}), bf16[8,24,7168]{2,1,0:T(8,128)(2,1)S(1)}, u32[]{:S(2)}, u32[]{:S(2)}) async-start(bf16[8,24,7168]{2,1,0:T(8,128)(2,1)} %bitcast.234), calls=%async_computation.1 | async-start | bytes 5505024 | tf_op jit(solution)/shard_map/all_to_all | solution.py:86
  160.3 1.5 copy-start.4
  160.7 15.9 %copy-start.8 = (f32[1,7168]{1,0:T(1,128)S(1)}, f32[1,7168]{1,0:T(1,128)}, u32[]{:S(2)}) copy-start(f32[1,7168]{1,0:T(1,128)} %param.19) | copy-start | bytes 86020
  163.5 12.8 %collective-permute-start = (bf16[32,7168]{1,0:T(8,128)(2,1)S(1)}, bf16[32,7168]{1,0:T(8,128)(2,1)S(1)}, u32[]{:S(2)}, u32[]{:S(2)}) collective-permute-start(bf16[32,7168]{1,0:T(8,128)(2,1)S(1)} %get-tuple-element.553), channel_id=1, source_target_pairs={{0,8},{8,16},{16,24},{1,9},{9,17},{17,25},{2,10},{10,18},{18,26},{... | collective-permute-start | bytes 1376264 | tf_op jit(solution)/shard_map/ppermute | solution.py:25
  177.3 66.2 %copy-start = (bf16[1,7168,256]{2,1,0:T(8,128)(2,1)S(1)}, bf16[1,7168,256]{2,1,0:T(8,128)(2,1)}, u32[]{:S(2)}) copy-start(bf16[1,7168,256]{2,1,0:T(8,128)(2,1)} %param.20) | copy-start | bytes 11010052
  252.3 66.6 %all-to-all-start.3 = ((bf16[8,24,7168]{2,1,0:T(8,128)(2,1)}), bf16[8,24,7168]{2,1,0:T(8,128)(2,1)S(1)}, u32[]{:S(2)}, u32[]{:S(2)}) async-start(bf16[8,24,7168]{2,1,0:T(8,128)(2,1)} %bitcast.238), calls=%async_computation.3 | async-start | bytes 5505024 | tf_op jit(solution)/shard_map/all_to_all | solution.py:86
  318.9 17.1 %copy-start.5 = (bf16[2,32,7168]{2,1,0:T(8,128)(2,1)S(1)}, bf16[2,32,7168]{2,1,0:T(8,128)(2,1)}, u32[]{:S(2)}) copy-start(bf16[2,32,7168]{2,1,0:T(8,128)(2,1)} %param.18) | copy-start | bytes 2752516
  322.1 13.9 %collective-permute-start.1 = (bf16[32,7168]{1,0:T(8,128)(2,1)S(1)}, bf16[32,7168]{1,0:T(8,128)(2,1)S(1)}, u32[]{:S(2)}, u32[]{:S(2)}) collective-permute-start(bf16[32,7168]{1,0:T(8,128)(2,1)S(1)} %get-tuple-element.555), channel_id=1, source_target_pairs={{0,8},{8,16},{16,24},{1,9},{9,17},{17,25},{2,10},{10,18},{18,26},{... | collective-permute-start | bytes 1376264 | tf_op jit(solution)/shard_map/ppermute | solution.py:25
  337.0 66.2 %copy-start.1 = (bf16[1,7168,256]{2,1,0:T(8,128)(2,1)S(1)}, bf16[1,7168,256]{2,1,0:T(8,128)(2,1)}, u32[]{:S(2)}) copy-start(bf16[1,7168,256]{2,1,0:T(8,128)(2,1)} %param.20) | copy-start | bytes 11010052
  412.0 66.6 %all-to-all-start.5 = ((bf16[8,24,7168]{2,1,0:T(8,128)(2,1)}), bf16[8,24,7168]{2,1,0:T(8,128)(2,1)S(1)}, u32[]{:S(2)}, u32[]{:S(2)}) async-start(bf16[8,24,7168]{2,1,0:T(8,128)(2,1)} %bitcast.239), calls=%async_computation.5 | async-start | bytes 5505024 | tf_op jit(solution)/shard_map/all_to_all | solution.py:86
  478.6 17.0 %copy-start.6 = (bf16[2,32,7168]{2,1,0:T(8,128)(2,1)S(1)}, bf16[2,32,7168]{2,1,0:T(8,128)(2,1)}, u32[]{:S(2)}) copy-start(bf16[2,32,7168]{2,1,0:T(8,128)(2,1)} %param.18) | copy-start | bytes 2752516
  481.8 13.8 %collective-permute-start.2 = (bf16[32,7168]{1,0:T(8,128)(2,1)S(1)}, bf16[32,7168]{1,0:T(8,128)(2,1)S(1)}, u32[]{:S(2)}, u32[]{:S(2)}) collective-permute-start(bf16[32,7168]{1,0:T(8,128)(2,1)S(1)} %get-tuple-element.557), channel_id=1, source_target_pairs={{0,8},{8,16},{16,24},{1,9},{9,17},{17,25},{2,10},{10,18},{18,26},{... | collective-permute-start | bytes 1376264 | tf_op jit(solution)/shard_map/ppermute | solution.py:25
  496.7 66.2 %copy-start.2 = (bf16[1,7168,256]{2,1,0:T(8,128)(2,1)S(1)}, bf16[1,7168,256]{2,1,0:T(8,128)(2,1)}, u32[]{:S(2)}) copy-start(bf16[1,7168,256]{2,1,0:T(8,128)(2,1)} %param.20) | copy-start | bytes 11010052
  571.6 66.6 %all-to-all-start.7 = ((bf16[8,24,7168]{2,1,0:T(8,128)(2,1)}), bf16[8,24,7168]{2,1,0:T(8,128)(2,1)S(1)}, u32[]{:S(2)}, u32[]{:S(2)}) async-start(bf16[8,24,7168]{2,1,0:T(8,128)(2,1)} %bitcast.237), calls=%async_computation.7 | async-start | bytes 5505024 | tf_op jit(solution)/shard_map/all_to_all | solution.py:86
  638.3 17.9 %copy-start.7 = (bf16[2,32,7168]{2,1,0:T(8,128)(2,1)S(1)}, bf16[2,32,7168]{2,1,0:T(8,128)(2,1)}, u32[]{:S(2)}) copy-start(bf16[2,32,7168]{2,1,0:T(8,128)(2,1)} %param.18) | copy-start | bytes 2752516
  641.4 14.7 %collective-permute-start.3 = (bf16[32,7168]{1,0:T(8,128)(2,1)S(1)}, bf16[32,7168]{1,0:T(8,128)(2,1)S(1)}, u32[]{:S(2)}, u32[]{:S(2)}) collective-permute-start(bf16[32,7168]{1,0:T(8,128)(2,1)S(1)} %get-tuple-element.559), channel_id=1, source_target_pairs={{0,8},{8,16},{16,24},{1,9},{9,17},{17,25},{2,10},{10,18},{18,26},{... | collective-permute-start | bytes 1376264 | tf_op jit(solution)/shard_map/ppermute | solution.py:25
  657.2 66.2 %copy-start.3 = (bf16[1,7168,256]{2,1,0:T(8,128)(2,1)S(1)}, bf16[1,7168,256]{2,1,0:T(8,128)(2,1)}, u32[]{:S(2)}) copy-start(bf16[1,7168,256]{2,1,0:T(8,128)(2,1)} %param.20) | copy-start | bytes 11010052
  732.1 66.6 %all-to-all-start.9 = ((bf16[8,24,7168]{2,1,0:T(8,128)(2,1)}), bf16[8,24,7168]{2,1,0:T(8,128)(2,1)S(1)}, u32[]{:S(2)}, u32[]{:S(2)}) async-start(bf16[8,24,7168]{2,1,0:T(8,128)(2,1)} %bitcast.236), calls=%async_computation.9 | async-start | bytes 5505024 | tf_op jit(solution)/shard_map/all_to_all | solution.py:86
  735.7 95.2 %reduce-scatter.2.cloned.1.call-start = ((), (), s32[]{:S(2)}) async-start(), calls=%async_computation.11 | async-start | bytes 1146880 | tf_op jit(solution)/shard_map/reduce_scatter | solution.py:132
Sparse Core Ops, SparseCore 0:
  802.1 28.8 reduce-scatter.1
where the time goes:
time: 839 us; the launch traced here: 838 us
  waiting for transfers between devices  379 us (45%)
  blocking collectives  325 us (39%)
  matrix products  61.6 us (7%)
  starting transfers between devices  42.3 us (5%)
  between operations  14.6 us (2%)
    all_to_all x5, waiting for transfers between devices, moe_layer(): lax.all_to_all(partials, 'expert', split_axis=0, concat_axis=0, tiled=True)  313 us
    all_to_all x4, blocking collectives, moe_layer(): lax.all_to_all(outgoing, 'expert', split_axis=0, concat_axis=0, tiled=True)  265 us
    unnamed x1, blocking collectives  60.4 us
    dot_general x5, matrix products, expert_rows(): jnp.dot(hidden, down_rows, preferred_element_type=jnp.float32)  38.9 us
    ppermute x4, waiting for transfers between devices, shifted(): return lax.ppermute(array, axis, pairs)  37.5 us
    reduce_scatter x1, waiting for transfers between devices, body(): lax.psum_scatter(results.astype(jnp.float32).astype(jnp.bfloat16), 'secti...  29 us
    all_to_all x5, starting transfers between devices, moe_layer(): lax.all_to_all(partials, 'expert', split_axis=0, concat_axis=0, tiled=True)  18.3 us
    ppermute x4, starting transfers between devices, shifted(): return lax.ppermute(array, axis, pairs)  17.4 us
  transfers between devices with their start and end apart: 11, of which 10 were waited for; matrix products, arithmetic and copies ran while one was open for 1% of the time, Pallas kernels for 0%

commit v1 on v0

--- a/solution.py
+++ b/solution.py
@@ -4,6 +4,29 @@
 from jax.sharding import PartitionSpec as P
 
 EPSILON = 1e-06
+
+
+def split_up(shard, dim, count):
+    shape = shard.shape
+    blocks = shard.reshape(*shape[:dim], count, shape[dim] // count, *shape[dim + 1 :])
+    return jnp.moveaxis(blocks, dim, 0)
+
+
+def joined_along(blocks, dim):
+    blocks = jnp.moveaxis(blocks, 0, dim)
+    shape = blocks.shape
+    return blocks.reshape(*shape[:dim], shape[dim] * shape[dim + 1], *shape[dim + 2 :])
+
+
+def rotated_exchange(shard, axis, split_dim, concat_dim):
+    length, index = (lax.axis_size(axis), lax.axis_index(axis))
+    pieces = split_up(shard, split_dim, length)
+    outs = [pieces[index]]
+    for step in range(1, length):
+        sent = pieces[(index + step) % length]
+        outs.append(lax.ppermute(sent, axis, [(i, (i + step) % length) for i in range(length)]))
+    pieces = jnp.stack(outs)[(index - jnp.arange(length)) % length]
+    return joined_along(pieces, concat_dim)
 
 
 def entering(array, axis, combine, identity):
@@ -78,10 +101,7 @@
     ).astype(jnp.bfloat16)
     outgoing = jnp.repeat(packed.reshape(expert_total, slot_count, width), split_count, axis=0)
     partials = expert_rows(
-        lax.all_to_all(outgoing, "expert", split_axis=0, concat_axis=0, tiled=True),
-        gate_cols,
-        up_cols,
-        down_rows,
+        rotated_exchange(outgoing, "expert", 0, 0), gate_cols, up_cols, down_rows
     )
     returned = lax.all_to_all(partials, "expert", split_axis=0, concat_axis=0, tiled=True)
     summed = jnp.sum(

time: 839 us -> 857 us (1.021)
  blocking collectives: 325 us -> 39.7 us
  waiting for transfers between devices: 379 us -> 518 us
  starting transfers between devices: 42.3 us -> 165 us
  local copies, waits for them, and re-layouts: 7 us -> 31.8 us
    all_to_all x4 -> x0, blocking collectives: 265 us -> none  [moe_layer(): lax.all_to_all(outgoing, 'expert', split_axis=0, concat_axis=0, tiled=True)]
    ppermute x0 -> x35, waiting for transfers between devices: none -> 139 us  [rotated_exchange(): lax.ppermute(sent, axis, [(i, (i + step) % length) for i in range(length)])]
    all_to_all x5, starting transfers between devices: 18.3 us -> 89.8 us  [moe_layer(): lax.all_to_all(partials, 'expert', split_axis=0, concat_axis=0, tiled=True)]
    ppermute x0 -> x35, starting transfers between devices: none -> 57.8 us  [rotated_exchange(): lax.ppermute(sent, axis, [(i, (i + step) % length) for i in range(length)])]
    unnamed x1, blocking collectives: 60.4 us -> 39.7 us
    gather x0 -> x5, local copies, waits for them, and re-layouts: none -> 12.5 us  [rotated_exchange(): pieces = jnp.stack(outs)[(index - jnp.arange(length)) % length]]
    unnamed x35 -> x67, local copies, waits for them, and re-layouts: 1.77 us -> 13.1 us
  transfers between devices with their start and end apart: 11 -> 45, of which waited for: 10 -> 32; matrix products, arithmetic and copies ran while one was open for 1% -> 1% of each run, Pallas kernels for 0% -> 0%
where the time goes in v1:
time: 857 us; the launch traced here: 848 us
  waiting for transfers between devices  518 us (60%)
  starting transfers between devices  165 us (19%)
  matrix products  69.6 us (8%)
  blocking collectives  39.7 us (5%)
  local copies, waits for them, and re-layouts  31.8 us (4%)
  between operations  15.3 us (2%)
    all_to_all x5, waiting for transfers between devices, moe_layer(): lax.all_to_all(partials, 'expert', split_axis=0, concat_axis=0, tiled=True)  313 us
    ppermute x35, waiting for transfers between devices, rotated_exchange(): lax.ppermute(sent, axis, [(i, (i + step) % length) for i in range(length)])  139 us
    all_to_all x5, starting transfers between devices, moe_layer(): lax.all_to_all(partials, 'expert', split_axis=0, concat_axis=0, tiled=True)  89.8 us
    ppermute x35, starting transfers between devices, rotated_exchange(): lax.ppermute(sent, axis, [(i, (i + step) % length) for i in range(length)])  57.8 us
    unnamed x1, blocking collectives  39.7 us
    dot_general x5, matrix products, expert_rows(): jnp.dot(hidden, down_rows, preferred_element_type=jnp.float32)  38.9 us
    ppermute x4, waiting for transfers between devices, shifted(): return lax.ppermute(array, axis, pairs)  37.5 us
    reduce_scatter x1, waiting for transfers between devices, body(): lax.psum_scatter(results.astype(jnp.float32).astype(jnp.bfloat16), 'secti...  29 us
  transfers between devices with their start and end apart: 45, of which 32 were waited for; matrix products, arithmetic and copies ran while one was open for 1% of the time, Pallas kernels for 0%

profile of v1, /device:TPU:0, one launch (start us, length us, event | category | flops | bytes accessed | tf_op | source)
XLA Modules:
  0.0 847.6 jit_solution(10725967930479506055)
XLA Ops:
  12.6 2.6 collective-permute-start.1
  15.2 2.6 collective-permute-start.2
  22.9 39.7 %all-reduce.5 = (s32[16]{0:T(128)S(1)}, s32[16]{0:T(128)S(1)}, s32[16]{0:T(128)S(1)}, s32[16]{0:T(128)S(1)}, s32[16]{0:T(128)S(1)}) all-reduce(s32[16]{0:T(128)S(1)} %dynamic-update-slice.9, s32[16]{0:T(128)S(1)} %dynamic-update-slice.6, s32[16]{0:T(128)S(1)} %dynamic-update-slice.7, ...), channel_id=6, replica_groups=mesh['section'=4,'expert'=8] {'expert'}, use_global_device_ids=true, to_apply=%add.4 | all-reduce | flops 80 | bytes 640
  63.5 5.8 collective-permute-start.5
  72.5 3.9 collective-permute-done.5
  76.4 3.7 collective-permute-done.6
  81.7 2.5 gather_fusion
  84.2 2.9 fusion.31
  87.1 7.8 convolution_convert_fusion.4
  94.9 5.0 all-to-all-start
  101.5 61.5 %all-to-all-done = bf16[8,24,7168]{2,1,0:T(8,128)(2,1)S(1)} async-done(((bf16[8,24,7168]{2,1,0:T(8,128)(2,1)}), bf16[8,24,7168]{2,1,0:T(8,128)(2,1)S(1)}, u32[]{:S(2)}, u32[]{:S(2)}) %all-to-all-start) | async-done | bytes 2752544 | tf_op jit(solution)/shard_map/all_to_all | solution.py:106
  166.2 3.4 collective-permute-start.7
  169.6 9.4 %collective-permute-done.7 = bf16[32,7168]{1,0:T(8,128)(2,1)S(1)} collective-permute-done((bf16[32,7168]{1,0:T(8,128)(2,1)S(1)}, bf16[32,7168]{1,0:T(8,128)(2,1)S(1)}, u32[]{:S(2)}, u32[]{:S(2)}) %collective-permute-start.7) | collective-permute-done | bytes 458784 | tf_op jit(solution)/shard_map/ppermute | solution.py:48
  180.4 2.3 collective-permute-start.10
  185.1 6.9 collective-permute-done.8
  193.3 6.3 collective-permute-start.14
  199.6 22.3 %collective-permute-done.10 = bf16[1,24,7168]{2,1,0:T(8,128)(2,1)S(1)} collective-permute-done((bf16[1,24,7168]{2,1,0:T(8,128)(2,1)S(1)}, bf16[1,24,7168]{2,1,0:T(8,128)(2,1)S(1)}, u32[]{:S(2)}, u32[]{:S(2)}) %collective-permute-start.10) | collective-permute-done | bytes 344096 | tf_op jit(solution)/shard_map/ppermute | solution.py:27
  222.2 2.0 collective-permute-done.14
  225.8 2.5 gather_fusion.1
  228.3 2.9 fusion.29
  231.2 7.8 convolution_convert_fusion.3
  239.0 21.2 %all-to-all-start.1 = ((bf16[8,24,7168]{2,1,0:T(8,128)(2,1)}), bf16[8,24,7168]{2,1,0:T(8,128)(2,1)S(1)}, u32[]{:S(2)}, u32[]{:S(2)}) async-start(bf16[8,24,7168]{2,1,0:T(8,128)(2,1)} %bitcast.384), calls=%async_computation.1 | async-start | bytes 5505024 | tf_op jit(solution)/shard_map/all_to_all | solution.py:106
  260.3 62.9 %all-to-all-done.1 = bf16[8,24,7168]{2,1,0:T(8,128)(2,1)S(1)} async-done(((bf16[8,24,7168]{2,1,0:T(8,128)(2,1)}), bf16[8,24,7168]{2,1,0:T(8,128)(2,1)S(1)}, u32[]{:S(2)}, u32[]{:S(2)}) %all-to-all-start.1) | async-done | bytes 2752544 | tf_op jit(solution)/shard_map/all_to_all | solution.py:106
  323.7 2.8 fusion.97
  326.5 4.4 collective-permute-start.15
  330.9 9.4 %collective-permute-done.15 = bf16[32,7168]{1,0:T(8,128)(2,1)S(1)} collective-permute-done((bf16[32,7168]{1,0:T(8,128)(2,1)S(1)}, bf16[32,7168]{1,0:T(8,128)(2,1)S(1)}, u32[]{:S(2)}, u32[]{:S(2)}) %collective-permute-start.15) | collective-permute-done | bytes 458784 | tf_op jit(solution)/shard_map/ppermute | solution.py:48
  341.8 2.4 collective-permute-start.18
  346.5 6.8 collective-permute-done.16
  354.7 6.0 collective-permute-start.22
  360.7 22.6 %collective-permute-done.18 = bf16[1,24,7168]{2,1,0:T(8,128)(2,1)S(1)} collective-permute-done((bf16[1,24,7168]{2,1,0:T(8,128)(2,1)S(1)}, bf16[1,24,7168]{2,1,0:T(8,128)(2,1)S(1)}, u32[]{:S(2)}, u32[]{:S(2)}) %collective-permute-start.18) | collective-permute-done | bytes 344096 | tf_op jit(solution)/shard_map/ppermute | solution.py:27
  383.6 2.0 collective-permute-done.22
  387.2 2.5 gather_fusion.2
  389.7 2.9 fusion.27
  392.6 7.8 convolution_convert_fusion.2
  400.4 21.3 %all-to-all-start.2 = ((bf16[8,24,7168]{2,1,0:T(8,128)(2,1)}), bf16[8,24,7168]{2,1,0:T(8,128)(2,1)S(1)}, u32[]{:S(2)}, u32[]{:S(2)}) async-start(bf16[8,24,7168]{2,1,0:T(8,128)(2,1)} %bitcast.385), calls=%async_computation.2 | async-start | bytes 5505024 | tf_op jit(solution)/shard_map/all_to_all | solution.py:106
  421.9 62.9 %all-to-all-done.2 = bf16[8,24,7168]{2,1,0:T(8,128)(2,1)S(1)} async-done(((bf16[8,24,7168]{2,1,0:T(8,128)(2,1)}), bf16[8,24,7168]{2,1,0:T(8,128)(2,1)S(1)}, u32[]{:S(2)}, u32[]{:S(2)}) %all-to-all-start.2) | async-done | bytes 2752544 | tf_op jit(solution)/shard_map/all_to_all | solution.py:106
  485.2 2.8 fusion.96
  488.0 4.4 collective-permute-start.23
  492.6 9.3 %collective-permute-done.23 = bf16[32,7168]{1,0:T(8,128)(2,1)S(1)} collective-permute-done((bf16[32,7168]{1,0:T(8,128)(2,1)S(1)}, bf16[32,7168]{1,0:T(8,128)(2,1)S(1)}, u32[]{:S(2)}, u32[]{:S(2)}) %collective-permute-start.23) | collective-permute-done | bytes 458784 | tf_op jit(solution)/shard_map/ppermute | solution.py:48
  503.2 2.4 collective-permute-start.26
  508.0 6.9 collective-permute-done.24
  516.2 6.0 collective-permute-start.30
  522.2 22.6 %collective-permute-done.26 = bf16[1,24,7168]{2,1,0:T(8,128)(2,1)S(1)} collective-permute-done((bf16[1,24,7168]{2,1,0:T(8,128)(2,1)S(1)}, bf16[1,24,7168]{2,1,0:T(8,128)(2,1)S(1)}, u32[]{:S(2)}, u32[]{:S(2)}) %collective-permute-start.26) | collective-permute-done | bytes 344096 | tf_op jit(solution)/shard_map/ppermute | solution.py:27
  545.1 2.0 collective-permute-done.30
  548.7 2.5 gather_fusion.3
  551.2 2.9 fusion.25
  554.1 7.8 convolution_convert_fusion.1
  561.9 21.1 %all-to-all-start.3 = ((bf16[8,24,7168]{2,1,0:T(8,128)(2,1)}), bf16[8,24,7168]{2,1,0:T(8,128)(2,1)S(1)}, u32[]{:S(2)}, u32[]{:S(2)}) async-start(bf16[8,24,7168]{2,1,0:T(8,128)(2,1)} %bitcast.383), calls=%async_computation.3 | async-start | bytes 5505024 | tf_op jit(solution)/shard_map/all_to_all | solution.py:106
  583.2 62.9 %all-to-all-done.3 = bf16[8,24,7168]{2,1,0:T(8,128)(2,1)S(1)} async-done(((bf16[8,24,7168]{2,1,0:T(8,128)(2,1)}), bf16[8,24,7168]{2,1,0:T(8,128)(2,1)S(1)}, u32[]{:S(2)}, u32[]{:S(2)}) %all-to-all-start.3) | async-done | bytes 2752544 | tf_op jit(solution)/shard_map/all_to_all | solution.py:106
  646.6 2.8 fusion.95
  649.3 5.2 collective-permute-start.31
  654.6 9.4 %collective-permute-done.31 = bf16[32,7168]{1,0:T(8,128)(2,1)S(1)} collective-permute-done((bf16[32,7168]{1,0:T(8,128)(2,1)S(1)}, bf16[32,7168]{1,0:T(8,128)(2,1)S(1)}, u32[]{:S(2)}, u32[]{:S(2)}) %collective-permute-start.31) | collective-permute-done | bytes 458784 | tf_op jit(solution)/shard_map/ppermute | solution.py:48
  665.4 2.4 collective-permute-start.34
  670.2 6.9 collective-permute-done.32
  678.3 6.2 collective-permute-start.38
  684.5 22.4 %collective-permute-done.34 = bf16[1,24,7168]{2,1,0:T(8,128)(2,1)S(1)} collective-permute-done((bf16[1,24,7168]{2,1,0:T(8,128)(2,1)S(1)}, bf16[1,24,7168]{2,1,0:T(8,128)(2,1)S(1)}, u32[]{:S(2)}, u32[]{:S(2)}) %collective-permute-start.34) | collective-permute-done | bytes 344096 | tf_op jit(solution)/shard_map/ppermute | solution.py:27
  707.2 2.0 collective-permute-done.38
  710.9 2.5 gather_fusion.4
  713.4 2.9 fusion.23
  716.3 7.8 convolution_convert_fusion
  724.1 21.1 %all-to-all-start.4 = ((bf16[8,24,7168]{2,1,0:T(8,128)(2,1)}), bf16[8,24,7168]{2,1,0:T(8,128)(2,1)S(1)}, u32[]{:S(2)}, u32[]{:S(2)}) async-start(bf16[8,24,7168]{2,1,0:T(8,128)(2,1)} %bitcast.382), calls=%async_computation.4 | async-start | bytes 5505024 | tf_op jit(solution)/shard_map/all_to_all | solution.py:106
  745.4 62.9 %all-to-all-done.4 = bf16[8,24,7168]{2,1,0:T(8,128)(2,1)S(1)} async-done(((bf16[8,24,7168]{2,1,0:T(8,128)(2,1)}), bf16[8,24,7168]{2,1,0:T(8,128)(2,1)S(1)}, u32[]{:S(2)}, u32[]{:S(2)}) %all-to-all-start.4) | async-done | bytes 2752544 | tf_op jit(solution)/shard_map/all_to_all | solution.py:106
  808.7 2.7 fusion.7
  811.5 29.0 %reduce-scatter.2.cloned.1.call-done = bf16[2,32,1792]{2,1,0:T(8,128)(2,1)} async-done(((bf16[2,32,7168]{2,1,0:T(8,128)(2,1)}), bf16[2,32,1792]{2,1,0:T(8,128)(2,1)}) %reduce-scatter.2.cloned.1.call-update) | async-done | bytes 229392 | tf_op jit(solution)/shard_map/reduce_scatter | solution.py:152
  (228 shorter events, 51.6 us)
Async XLA Ops:
  10.6 9.8 %copy-start.12 = (u32[32]{0:T(128)S(1)}, u32[32]{0:T(128)}, u32[]{:S(2)}) copy-start(u32[32]{0:T(128)} %constant.346) | copy-start | bytes 388
  12.1 51.4 %collective-permute-start = (bf16[1,24,7168]{2,1,0:T(8,128)(2,1)}, bf16[1,24,7168]{2,1,0:T(8,128)(2,1)}, u32[]{:S(2)}, u32[]{:S(2)}) collective-permute-start(bf16[1,24,7168]{2,1,0:T(8,128)(2,1)} %get-tuple-element.581), channel_id=1, source_target_pairs={{0,1},{1,2},{2,3},{3,4},{4,5},{5,6},{6,7},{7,0},{8,9},{9,10},{10,1... | collective-permute-start | bytes 1032200 | tf_op jit(solution)/shard_map/ppermute | solution.py:27
  12.6 57.7 %collective-permute-start.1 = (bf16[1,24,7168]{2,1,0:T(8,128)(2,1)}, bf16[1,24,7168]{2,1,0:T(8,128)(2,1)}, u32[]{:S(2)}, u32[]{:S(2)}) collective-permute-start(bf16[1,24,7168]{2,1,0:T(8,128)(2,1)} %get-tuple-element.580), channel_id=1, source_target_pairs={{0,2},{1,3},{2,4},{3,5},{4,6},{5,7},{6,0},{7,1},{8,10},{9,11},{10,... | collective-permute-start | bytes 1032200 | tf_op jit(solution)/shard_map/ppermute | solution.py:27
  15.2 56.3 %collective-permute-start.2 = (bf16[1,24,7168]{2,1,0:T(8,128)(2,1)}, bf16[1,24,7168]{2,1,0:T(8,128)(2,1)}, u32[]{:S(2)}, u32[]{:S(2)}) collective-permute-start(bf16[1,24,7168]{2,1,0:T(8,128)(2,1)} %get-tuple-element.579), channel_id=1, source_target_pairs={{0,3},{1,4},{2,5},{3,6},{4,7},{5,0},{6,1},{7,2},{8,11},{9,12},{10,... | collective-permute-start | bytes 1032200 | tf_op jit(solution)/shard_map/ppermute | solution.py:27
  17.8 54.7 %collective-permute-start.3 = (bf16[1,24,7168]{2,1,0:T(8,128)(2,1)}, bf16[1,24,7168]{2,1,0:T(8,128)(2,1)S(1)}, u32[]{:S(2)}, u32[]{:S(2)}) collective-permute-start(bf16[1,24,7168]{2,1,0:T(8,128)(2,1)} %get-tuple-element.578), channel_id=1, source_target_pairs={{0,4},{1,5},{2,6},{3,7},{4,0},{5,1},{6,2},{7,3},{8,12},{9,13},{10,... | collective-permute-start | bytes 1032200 | tf_op jit(solution)/shard_map/ppermute | solution.py:27
  19.0 53.5 %collective-permute-start.4 = (bf16[1,24,7168]{2,1,0:T(8,128)(2,1)}, bf16[1,24,7168]{2,1,0:T(8,128)(2,1)S(1)}, u32[]{:S(2)}, u32[]{:S(2)}) collective-permute-start(bf16[1,24,7168]{2,1,0:T(8,128)(2,1)} %get-tuple-element.577), channel_id=1, source_target_pairs={{0,5},{1,6},{2,7},{3,0},{4,1},{5,2},{6,3},{7,4},{8,13},{9,14},{10,... | collective-permute-start | bytes 1032200 | tf_op jit(solution)/shard_map/ppermute | solution.py:27
  63.5 12.9 %collective-permute-start.5 = (bf16[1,24,7168]{2,1,0:T(8,128)(2,1)}, bf16[1,24,7168]{2,1,0:T(8,128)(2,1)S(1)}, u32[]{:S(2)}, u32[]{:S(2)}) collective-permute-start(bf16[1,24,7168]{2,1,0:T(8,128)(2,1)} %get-tuple-element.576), channel_id=1, source_target_pairs={{0,6},{1,7},{2,0},{3,1},{4,2},{5,3},{6,4},{7,5},{8,14},{9,15},{10,... | collective-permute-start | bytes 1032200 | tf_op jit(solution)/shard_map/ppermute | solution.py:27
  70.4 9.7 %collective-permute-start.6 = (bf16[1,24,7168]{2,1,0:T(8,128)(2,1)}, bf16[1,24,7168]{2,1,0:T(8,128)(2,1)S(1)}, u32[]{:S(2)}, u32[]{:S(2)}) collective-permute-start(bf16[1,24,7168]{2,1,0:T(8,128)(2,1)} %get-tuple-element.575), channel_id=1, source_target_pairs={{0,7},{1,0},{2,1},{3,2},{4,3},{5,4},{6,5},{7,6},{8,15},{9,8},{10,9... | collective-permute-start | bytes 1032200 | tf_op jit(solution)/shard_map/ppermute | solution.py:27
  80.1 1.6 copy-start.4
  94.9 6.3 copy-start.11
  94.9 6.4 copy-start.10
  94.9 68.1 %all-to-all-start = ((bf16[8,24,7168]{2,1,0:T(8,128)(2,1)}), bf16[8,24,7168]{2,1,0:T(8,128)(2,1)S(1)}, u32[]{:S(2)}, u32[]{:S(2)}) async-start(bf16[8,24,7168]{2,1,0:T(8,128)(2,1)} %bitcast.381), calls=%async_computation | async-start | bytes 5505024 | tf_op jit(solution)/shard_map/all_to_all | solution.py:106
  163.0 1.5 copy-start
  163.4 15.9 %copy-start.9 = (f32[1,7168]{1,0:T(1,128)S(1)}, f32[1,7168]{1,0:T(1,128)}, u32[]{:S(2)}) copy-start(f32[1,7168]{1,0:T(1,128)} %param.19) | copy-start | bytes 86020
  166.2 12.8 %collective-permute-start.7 = (bf16[32,7168]{1,0:T(8,128)(2,1)S(1)}, bf16[32,7168]{1,0:T(8,128)(2,1)S(1)}, u32[]{:S(2)}, u32[]{:S(2)}) collective-permute-start(bf16[32,7168]{1,0:T(8,128)(2,1)S(1)} %get-tuple-element.593), channel_id=1, source_target_pairs={{0,8},{8,16},{16,24},{1,9},{9,17},{17,25},{2,10},{10,18},{18,26},{... | collective-permute-start | bytes 1376264 | tf_op jit(solution)/shard_map/ppermute | solution.py:48
  180.3 11.8 %collective-permute-start.8 = (bf16[1,24,7168]{2,1,0:T(8,128)(2,1)S(1)}, bf16[1,24,7168]{2,1,0:T(8,128)(2,1)S(1)}, u32[]{:S(2)}, u32[]{:S(2)}) collective-permute-start(bf16[1,24,7168]{2,1,0:T(8,128)(2,1)S(1)} %get-tuple-element.573), channel_id=1, source_target_pairs={{0,1},{1,2},{2,3},{3,4},{4,5},{5,6},{6,7},{7,0},{8,9},{9,10},{10,1... | collective-permute-start | bytes 1032200 | tf_op jit(solution)/shard_map/ppermute | solution.py:27
  180.3 13.0 %collective-permute-start.9 = (bf16[1,24,7168]{2,1,0:T(8,128)(2,1)S(1)}, bf16[1,24,7168]{2,1,0:T(8,128)(2,1)S(1)}, u32[]{:S(2)}, u32[]{:S(2)}) collective-permute-start(bf16[1,24,7168]{2,1,0:T(8,128)(2,1)S(1)} %get-tuple-element.572), channel_id=1, source_target_pairs={{0,2},{1,3},{2,4},{3,5},{4,6},{5,7},{6,0},{7,1},{8,10},{9,11},{10,... | collective-permute-start | bytes 1032200 | tf_op jit(solution)/shard_map/ppermute | solution.py:27
  180.4 41.5 %collective-permute-start.10 = (bf16[1,24,7168]{2,1,0:T(8,128)(2,1)S(1)}, bf16[1,24,7168]{2,1,0:T(8,128)(2,1)S(1)}, u32[]{:S(2)}, u32[]{:S(2)}) collective-permute-start(bf16[1,24,7168]{2,1,0:T(8,128)(2,1)S(1)} %get-tuple-element.571), channel_id=1, source_target_pairs={{0,3},{1,4},{2,5},{3,6},{4,7},{5,0},{6,1},{7,2},{8,11},{9,12},{10,... | collective-permute-start | bytes 1032200 | tf_op jit(solution)/shard_map/ppermute | solution.py:27
  182.7 39.4 %collective-permute-start.11 = (bf16[1,24,7168]{2,1,0:T(8,128)(2,1)S(1)}, bf16[1,24,7168]{2,1,0:T(8,128)(2,1)S(1)}, u32[]{:S(2)}, u32[]{:S(2)}) collective-permute-start(bf16[1,24,7168]{2,1,0:T(8,128)(2,1)S(1)} %get-tuple-element.570), channel_id=1, source_target_pairs={{0,4},{1,5},{2,6},{3,7},{4,0},{5,1},{6,2},{7,3},{8,12},{9,13},{10,... | collective-permute-start | bytes 1032200 | tf_op jit(solution)/shard_map/ppermute | solution.py:27
  184.4 37.7 %collective-permute-start.12 = (bf16[1,24,7168]{2,1,0:T(8,128)(2,1)S(1)}, bf16[1,24,7168]{2,1,0:T(8,128)(2,1)S(1)}, u32[]{:S(2)}, u32[]{:S(2)}) collective-permute-start(bf16[1,24,7168]{2,1,0:T(8,128)(2,1)S(1)} %get-tuple-element.569), channel_id=1, source_target_pairs={{0,5},{1,6},{2,7},{3,0},{4,1},{5,2},{6,3},{7,4},{8,13},{9,14},{10,... | collective-permute-start | bytes 1032200 | tf_op jit(solution)/shard_map/ppermute | solution.py:27
  192.0 30.1 %collective-permute-start.13 = (bf16[1,24,7168]{2,1,0:T(8,128)(2,1)S(1)}, bf16[1,24,7168]{2,1,0:T(8,128)(2,1)S(1)}, u32[]{:S(2)}, u32[]{:S(2)}) collective-permute-start(bf16[1,24,7168]{2,1,0:T(8,128)(2,1)S(1)} %get-tuple-element.568), channel_id=1, source_target_pairs={{0,6},{1,7},{2,0},{3,1},{4,2},{5,3},{6,4},{7,5},{8,14},{9,15},{10,... | collective-permute-start | bytes 1032200 | tf_op jit(solution)/shard_map/ppermute | solution.py:27
  193.3 30.9 %collective-permute-start.14 = (bf16[1,24,7168]{2,1,0:T(8,128)(2,1)S(1)}, bf16[1,24,7168]{2,1,0:T(8,128)(2,1)S(1)}, u32[]{:S(2)}, u32[]{:S(2)}) collective-permute-start(bf16[1,24,7168]{2,1,0:T(8,128)(2,1)S(1)} %get-tuple-element.567), channel_id=1, source_target_pairs={{0,7},{1,0},{2,1},{3,2},{4,3},{5,4},{6,5},{7,6},{8,15},{9,8},{10,9... | collective-permute-start | bytes 1032200 | tf_op jit(solution)/shard_map/ppermute | solution.py:27
  224.2 1.6 copy-start.6
  239.0 84.3 %all-to-all-start.1 = ((bf16[8,24,7168]{2,1,0:T(8,128)(2,1)}), bf16[8,24,7168]{2,1,0:T(8,128)(2,1)S(1)}, u32[]{:S(2)}, u32[]{:S(2)}) async-start(bf16[8,24,7168]{2,1,0:T(8,128)(2,1)} %bitcast.384), calls=%async_computation.1 | async-start | bytes 5505024 | tf_op jit(solution)/shard_map/all_to_all | solution.py:106
  323.3 17.1 %copy-start.1 = (bf16[2,32,7168]{2,1,0:T(8,128)(2,1)S(1)}, bf16[2,32,7168]{2,1,0:T(8,128)(2,1)}, u32[]{:S(2)}) copy-start(bf16[2,32,7168]{2,1,0:T(8,128)(2,1)} %param.18) | copy-start | bytes 2752516
  326.5 13.9 %collective-permute-start.15 = (bf16[32,7168]{1,0:T(8,128)(2,1)S(1)}, bf16[32,7168]{1,0:T(8,128)(2,1)S(1)}, u32[]{:S(2)}, u32[]{:S(2)}) collective-permute-start(bf16[32,7168]{1,0:T(8,128)(2,1)S(1)} %get-tuple-element.595), channel_id=1, source_target_pairs={{0,8},{8,16},{16,24},{1,9},{9,17},{17,25},{2,10},{10,18},{18,26},{... | collective-permute-start | bytes 1376264 | tf_op jit(solution)/shard_map/ppermute | solution.py:48
  341.6 11.8 %collective-permute-start.16 = (bf16[1,24,7168]{2,1,0:T(8,128)(2,1)S(1)}, bf16[1,24,7168]{2,1,0:T(8,128)(2,1)S(1)}, u32[]{:S(2)}, u32[]{:S(2)}) collective-permute-start(bf16[1,24,7168]{2,1,0:T(8,128)(2,1)S(1)} %get-tuple-element.565), channel_id=1, source_target_pairs={{0,1},{1,2},{2,3},{3,4},{4,5},{5,6},{6,7},{7,0},{8,9},{9,10},{10,1... | collective-permute-start | bytes 1032200 | tf_op jit(solution)/shard_map/ppermute | solution.py:27
  341.7 13.0 %collective-permute-start.17 = (bf16[1,24,7168]{2,1,0:T(8,128)(2,1)S(1)}, bf16[1,24,7168]{2,1,0:T(8,128)(2,1)S(1)}, u32[]{:S(2)}, u32[]{:S(2)}) collective-permute-start(bf16[1,24,7168]{2,1,0:T(8,128)(2,1)S(1)} %get-tuple-element.564), channel_id=1, source_target_pairs={{0,2},{1,3},{2,4},{3,5},{4,6},{5,7},{6,0},{7,1},{8,10},{9,11},{10,... | collective-permute-start | bytes 1032200 | tf_op jit(solution)/shard_map/ppermute | solution.py:27
  341.8 41.5 %collective-permute-start.18 = (bf16[1,24,7168]{2,1,0:T(8,128)(2,1)S(1)}, bf16[1,24,7168]{2,1,0:T(8,128)(2,1)S(1)}, u32[]{:S(2)}, u32[]{:S(2)}) collective-permute-start(bf16[1,24,7168]{2,1,0:T(8,128)(2,1)S(1)} %get-tuple-element.563), channel_id=1, source_target_pairs={{0,3},{1,4},{2,5},{3,6},{4,7},{5,0},{6,1},{7,2},{8,11},{9,12},{10,... | collective-permute-start | bytes 1032200 | tf_op jit(solution)/shard_map/ppermute | solution.py:27
  344.1 39.4 %collective-permute-start.19 = (bf16[1,24,7168]{2,1,0:T(8,128)(2,1)S(1)}, bf16[1,24,7168]{2,1,0:T(8,128)(2,1)S(1)}, u32[]{:S(2)}, u32[]{:S(2)}) collective-permute-start(bf16[1,24,7168]{2,1,0:T(8,128)(2,1)S(1)} %get-tuple-element.562), channel_id=1, source_target_pairs={{0,4},{1,5},{2,6},{3,7},{4,0},{5,1},{6,2},{7,3},{8,12},{9,13},{10,... | collective-permute-start | bytes 1032200 | tf_op jit(solution)/shard_map/ppermute | solution.py:27
  345.8 37.7 %collective-permute-start.20 = (bf16[1,24,7168]{2,1,0:T(8,128)(2,1)S(1)}, bf16[1,24,7168]{2,1,0:T(8,128)(2,1)S(1)}, u32[]{:S(2)}, u32[]{:S(2)}) collective-permute-start(bf16[1,24,7168]{2,1,0:T(8,128)(2,1)S(1)} %get-tuple-element.561), channel_id=1, source_target_pairs={{0,5},{1,6},{2,7},{3,0},{4,1},{5,2},{6,3},{7,4},{8,13},{9,14},{10,... | collective-permute-start | bytes 1032200 | tf_op jit(solution)/shard_map/ppermute | solution.py:27
  353.4 30.1 %collective-permute-start.21 = (bf16[1,24,7168]{2,1,0:T(8,128)(2,1)S(1)}, bf16[1,24,7168]{2,1,0:T(8,128)(2,1)S(1)}, u32[]{:S(2)}, u32[]{:S(2)}) collective-permute-start(bf16[1,24,7168]{2,1,0:T(8,128)(2,1)S(1)} %get-tuple-element.560), channel_id=1, source_target_pairs={{0,6},{1,7},{2,0},{3,1},{4,2},{5,3},{6,4},{7,5},{8,14},{9,15},{10,... | collective-permute-start | bytes 1032200 | tf_op jit(solution)/shard_map/ppermute | solution.py:27
  354.7 31.0 %collective-permute-start.22 = (bf16[1,24,7168]{2,1,0:T(8,128)(2,1)S(1)}, bf16[1,24,7168]{2,1,0:T(8,128)(2,1)S(1)}, u32[]{:S(2)}, u32[]{:S(2)}) collective-permute-start(bf16[1,24,7168]{2,1,0:T(8,128)(2,1)S(1)} %get-tuple-element.559), channel_id=1, source_target_pairs={{0,7},{1,0},{2,1},{3,2},{4,3},{5,4},{6,5},{7,6},{8,15},{9,8},{10,9... | collective-permute-start | bytes 1032200 | tf_op jit(solution)/shard_map/ppermute | solution.py:27
  385.6 1.6 copy-start.7
  400.4 84.4 %all-to-all-start.2 = ((bf16[8,24,7168]{2,1,0:T(8,128)(2,1)}), bf16[8,24,7168]{2,1,0:T(8,128)(2,1)S(1)}, u32[]{:S(2)}, u32[]{:S(2)}) async-start(bf16[8,24,7168]{2,1,0:T(8,128)(2,1)} %bitcast.385), calls=%async_computation.2 | async-start | bytes 5505024 | tf_op jit(solution)/shard_map/all_to_all | solution.py:106
  484.8 17.0 %copy-start.2 = (bf16[2,32,7168]{2,1,0:T(8,128)(2,1)S(1)}, bf16[2,32,7168]{2,1,0:T(8,128)(2,1)}, u32[]{:S(2)}) copy-start(bf16[2,32,7168]{2,1,0:T(8,128)(2,1)} %param.18) | copy-start | bytes 2752516
  488.0 13.8 %collective-permute-start.23 = (bf16[32,7168]{1,0:T(8,128)(2,1)S(1)}, bf16[32,7168]{1,0:T(8,128)(2,1)S(1)}, u32[]{:S(2)}, u32[]{:S(2)}) collective-permute-start(bf16[32,7168]{1,0:T(8,128)(2,1)S(1)} %get-tuple-element.597), channel_id=1, source_target_pairs={{0,8},{8,16},{16,24},{1,9},{9,17},{17,25},{2,10},{10,18},{18,26},{... | collective-permute-start | bytes 1376264 | tf_op jit(solution)/shard_map/ppermute | solution.py:48
  503.1 11.8 %collective-permute-start.24 = (bf16[1,24,7168]{2,1,0:T(8,128)(2,1)S(1)}, bf16[1,24,7168]{2,1,0:T(8,128)(2,1)S(1)}, u32[]{:S(2)}, u32[]{:S(2)}) collective-permute-start(bf16[1,24,7168]{2,1,0:T(8,128)(2,1)S(1)} %get-tuple-element.557), channel_id=1, source_target_pairs={{0,1},{1,2},{2,3},{3,4},{4,5},{5,6},{6,7},{7,0},{8,9},{9,10},{10,1... | collective-permute-start | bytes 1032200 | tf_op jit(solution)/shard_map/ppermute | solution.py:27
  503.2 13.0 %collective-permute-start.25 = (bf16[1,24,7168]{2,1,0:T(8,128)(2,1)S(1)}, bf16[1,24,7168]{2,1,0:T(8,128)(2,1)S(1)}, u32[]{:S(2)}, u32[]{:S(2)}) collective-permute-start(bf16[1,24,7168]{2,1,0:T(8,128)(2,1)S(1)} %get-tuple-element.556), channel_id=1, source_target_pairs={{0,2},{1,3},{2,4},{3,5},{4,6},{5,7},{6,0},{7,1},{8,10},{9,11},{10,... | collective-permute-start | bytes 1032200 | tf_op jit(solution)/shard_map/ppermute | solution.py:27
  503.2 41.5 %collective-permute-start.26 = (bf16[1,24,7168]{2,1,0:T(8,128)(2,1)S(1)}, bf16[1,24,7168]{2,1,0:T(8,128)(2,1)S(1)}, u32[]{:S(2)}, u32[]{:S(2)}) collective-permute-start(bf16[1,24,7168]{2,1,0:T(8,128)(2,1)S(1)} %get-tuple-element.555), channel_id=1, source_target_pairs={{0,3},{1,4},{2,5},{3,6},{4,7},{5,0},{6,1},{7,2},{8,11},{9,12},{10,... | collective-permute-start | bytes 1032200 | tf_op jit(solution)/shard_map/ppermute | solution.py:27
  505.6 39.4 %collective-permute-start.27 = (bf16[1,24,7168]{2,1,0:T(8,128)(2,1)S(1)}, bf16[1,24,7168]{2,1,0:T(8,128)(2,1)S(1)}, u32[]{:S(2)}, u32[]{:S(2)}) collective-permute-start(bf16[1,24,7168]{2,1,0:T(8,128)(2,1)S(1)} %get-tuple-element.554), channel_id=1, source_target_pairs={{0,4},{1,5},{2,6},{3,7},{4,0},{5,1},{6,2},{7,3},{8,12},{9,13},{10,... | collective-permute-start | bytes 1032200 | tf_op jit(solution)/shard_map/ppermute | solution.py:27
  507.3 37.7 %collective-permute-start.28 = (bf16[1,24,7168]{2,1,0:T(8,128)(2,1)S(1)}, bf16[1,24,7168]{2,1,0:T(8,128)(2,1)S(1)}, u32[]{:S(2)}, u32[]{:S(2)}) collective-permute-start(bf16[1,24,7168]{2,1,0:T(8,128)(2,1)S(1)} %get-tuple-element.553), channel_id=1, source_target_pairs={{0,5},{1,6},{2,7},{3,0},{4,1},{5,2},{6,3},{7,4},{8,13},{9,14},{10,... | collective-permute-start | bytes 1032200 | tf_op jit(solution)/shard_map/ppermute | solution.py:27
  514.9 30.1 %collective-permute-start.29 = (bf16[1,24,7168]{2,1,0:T(8,128)(2,1)S(1)}, bf16[1,24,7168]{2,1,0:T(8,128)(2,1)S(1)}, u32[]{:S(2)}, u32[]{:S(2)}) collective-permute-start(bf16[1,24,7168]{2,1,0:T(8,128)(2,1)S(1)} %get-tuple-element.552), channel_id=1, source_target_pairs={{0,6},{1,7},{2,0},{3,1},{4,2},{5,3},{6,4},{7,5},{8,14},{9,15},{10,... | collective-permute-start | bytes 1032200 | tf_op jit(solution)/shard_map/ppermute | solution.py:27
  516.2 30.9 %collective-permute-start.30 = (bf16[1,24,7168]{2,1,0:T(8,128)(2,1)S(1)}, bf16[1,24,7168]{2,1,0:T(8,128)(2,1)S(1)}, u32[]{:S(2)}, u32[]{:S(2)}) collective-permute-start(bf16[1,24,7168]{2,1,0:T(8,128)(2,1)S(1)} %get-tuple-element.551), channel_id=1, source_target_pairs={{0,7},{1,0},{2,1},{3,2},{4,3},{5,4},{6,5},{7,6},{8,15},{9,8},{10,9... | collective-permute-start | bytes 1032200 | tf_op jit(solution)/shard_map/ppermute | solution.py:27
  547.1 1.6 copy-start.8
  561.9 84.2 %all-to-all-start.3 = ((bf16[8,24,7168]{2,1,0:T(8,128)(2,1)}), bf16[8,24,7168]{2,1,0:T(8,128)(2,1)S(1)}, u32[]{:S(2)}, u32[]{:S(2)}) async-start(bf16[8,24,7168]{2,1,0:T(8,128)(2,1)} %bitcast.383), calls=%async_computation.3 | async-start | bytes 5505024 | tf_op jit(solution)/shard_map/all_to_all | solution.py:106
  646.1 17.9 %copy-start.3 = (bf16[2,32,7168]{2,1,0:T(8,128)(2,1)S(1)}, bf16[2,32,7168]{2,1,0:T(8,128)(2,1)}, u32[]{:S(2)}) copy-start(bf16[2,32,7168]{2,1,0:T(8,128)(2,1)} %param.18) | copy-start | bytes 2752516
  649.3 14.7 %collective-permute-start.31 = (bf16[32,7168]{1,0:T(8,128)(2,1)S(1)}, bf16[32,7168]{1,0:T(8,128)(2,1)S(1)}, u32[]{:S(2)}, u32[]{:S(2)}) collective-permute-start(bf16[32,7168]{1,0:T(8,128)(2,1)S(1)} %get-tuple-element.599), channel_id=1, source_target_pairs={{0,8},{8,16},{16,24},{1,9},{9,17},{17,25},{2,10},{10,18},{18,26},{... | collective-permute-start | bytes 1376264 | tf_op jit(solution)/shard_map/ppermute | solution.py:48
  665.3 11.8 %collective-permute-start.32 = (bf16[1,24,7168]{2,1,0:T(8,128)(2,1)S(1)}, bf16[1,24,7168]{2,1,0:T(8,128)(2,1)S(1)}, u32[]{:S(2)}, u32[]{:S(2)}) collective-permute-start(bf16[1,24,7168]{2,1,0:T(8,128)(2,1)S(1)} %get-tuple-element.549), channel_id=1, source_target_pairs={{0,1},{1,2},{2,3},{3,4},{4,5},{5,6},{6,7},{7,0},{8,9},{9,10},{10,1... | collective-permute-start | bytes 1032200 | tf_op jit(solution)/shard_map/ppermute | solution.py:27
  665.3 13.0 %collective-permute-start.33 = (bf16[1,24,7168]{2,1,0:T(8,128)(2,1)S(1)}, bf16[1,24,7168]{2,1,0:T(8,128)(2,1)S(1)}, u32[]{:S(2)}, u32[]{:S(2)}) collective-permute-start(bf16[1,24,7168]{2,1,0:T(8,128)(2,1)S(1)} %get-tuple-element.548), channel_id=1, source_target_pairs={{0,2},{1,3},{2,4},{3,5},{4,6},{5,7},{6,0},{7,1},{8,10},{9,11},{10,... | collective-permute-start | bytes 1032200 | tf_op jit(solution)/shard_map/ppermute | solution.py:27
  665.4 41.5 %collective-permute-start.34 = (bf16[1,24,7168]{2,1,0:T(8,128)(2,1)S(1)}, bf16[1,24,7168]{2,1,0:T(8,128)(2,1)S(1)}, u32[]{:S(2)}, u32[]{:S(2)}) collective-permute-start(bf16[1,24,7168]{2,1,0:T(8,128)(2,1)S(1)} %get-tuple-element.547), channel_id=1, source_target_pairs={{0,3},{1,4},{2,5},{3,6},{4,7},{5,0},{6,1},{7,2},{8,11},{9,12},{10,... | collective-permute-start | bytes 1032200 | tf_op jit(solution)/shard_map/ppermute | solution.py:27
  667.8 39.4 %collective-permute-start.35 = (bf16[1,24,7168]{2,1,0:T(8,128)(2,1)S(1)}, bf16[1,24,7168]{2,1,0:T(8,128)(2,1)S(1)}, u32[]{:S(2)}, u32[]{:S(2)}) collective-permute-start(bf16[1,24,7168]{2,1,0:T(8,128)(2,1)S(1)} %get-tuple-element.546), channel_id=1, source_target_pairs={{0,4},{1,5},{2,6},{3,7},{4,0},{5,1},{6,2},{7,3},{8,12},{9,13},{10,... | collective-permute-start | bytes 1032200 | tf_op jit(solution)/shard_map/ppermute | solution.py:27
  669.4 37.7 %collective-permute-start.36 = (bf16[1,24,7168]{2,1,0:T(8,128)(2,1)S(1)}, bf16[1,24,7168]{2,1,0:T(8,128)(2,1)S(1)}, u32[]{:S(2)}, u32[]{:S(2)}) collective-permute-start(bf16[1,24,7168]{2,1,0:T(8,128)(2,1)S(1)} %get-tuple-element.545), channel_id=1, source_target_pairs={{0,5},{1,6},{2,7},{3,0},{4,1},{5,2},{6,3},{7,4},{8,13},{9,14},{10,... | collective-permute-start | bytes 1032200 | tf_op jit(solution)/shard_map/ppermute | solution.py:27
  677.0 30.1 %collective-permute-start.37 = (bf16[1,24,7168]{2,1,0:T(8,128)(2,1)S(1)}, bf16[1,24,7168]{2,1,0:T(8,128)(2,1)S(1)}, u32[]{:S(2)}, u32[]{:S(2)}) collective-permute-start(bf16[1,24,7168]{2,1,0:T(8,128)(2,1)S(1)} %get-tuple-element.544), channel_id=1, source_target_pairs={{0,6},{1,7},{2,0},{3,1},{4,2},{5,3},{6,4},{7,5},{8,14},{9,15},{10,... | collective-permute-start | bytes 1032200 | tf_op jit(solution)/shard_map/ppermute | solution.py:27
  678.3 31.0 %collective-permute-start.38 = (bf16[1,24,7168]{2,1,0:T(8,128)(2,1)S(1)}, bf16[1,24,7168]{2,1,0:T(8,128)(2,1)S(1)}, u32[]{:S(2)}, u32[]{:S(2)}) collective-permute-start(bf16[1,24,7168]{2,1,0:T(8,128)(2,1)S(1)} %get-tuple-element.543), channel_id=1, source_target_pairs={{0,7},{1,0},{2,1},{3,2},{4,3},{5,4},{6,5},{7,6},{8,15},{9,8},{10,9... | collective-permute-start | bytes 1032200 | tf_op jit(solution)/shard_map/ppermute | solution.py:27
  709.3 1.6 copy-start.5
  724.1 84.2 %all-to-all-start.4 = ((bf16[8,24,7168]{2,1,0:T(8,128)(2,1)}), bf16[8,24,7168]{2,1,0:T(8,128)(2,1)S(1)}, u32[]{:S(2)}, u32[]{:S(2)}) async-start(bf16[8,24,7168]{2,1,0:T(8,128)(2,1)} %bitcast.382), calls=%async_computation.4 | async-start | bytes 5505024 | tf_op jit(solution)/shard_map/all_to_all | solution.py:106
  745.2 95.3 %reduce-scatter.2.cloned.1.call-start = ((), (), s32[]{:S(2)}) async-start(), calls=%async_computation.6 | async-start | bytes 1146880 | tf_op jit(solution)/shard_map/reduce_scatter | solution.py:152
Sparse Core Ops, SparseCore 0:
  811.6 28.8 reduce-scatter.1
